TPU v7x, 512 devices: a whole 4x8x8 slice. The times are simulated.
512 devices in a mesh: group: 16 (over y, core), inner: 32 (over x, z).
Axes of the slice: x: 4, y: 8, z: 8, core: 2. Of those that a mesh axis runs over, the one named last changes fastest.
Arguments:
- pair_rows: bfloat16 [8192, 2048], P(('group', 'inner')), may hold values from -6 to 6
- group_ids: int32 [8192, 1], P(('group', 'inner')), may hold values from 0 to 15; in each aligned block of 16 rows (0 to 15, 16 to 31, ...) at most 2 rows name the same one
- local_ids: int32 [8192, 1], P(('group', 'inner')), may hold values from 0 to 1
- route_weight: float32 [8192], P(('group', 'inner')), may hold values from 0.3 to 1
- w_up: bfloat16 [32, 2048, 8192], P('group', None, 'inner'), may hold values from -0.125 to 0.125
- w_down: bfloat16 [32, 8192, 2048], P('group', 'inner'), may hold values from -0.0625 to 0.0625
Outputs:
- mixed: bfloat16 [8192, 2048], P(('group', 'inner'))
Inputs may be any that keep to these rules, and one draw needn't show every extreme that they name: `group_ids`: among the rows of one device no value is named more than 2 times, a bound that some block reaches.
All inputs are finite; a program needn't handle non-finite values.
Results may differ from a plain program's by a relative error of at most 0.02.
Values may be sent and summed in bfloat16 or wider, within the bound.
A program may use at most 64 MiB of HBM per device.

v0:
```python
import jax
import jax.numpy as jnp
from jax import lax
from jax.sharding import PartitionSpec as P


def body(pair_rows, group_ids, local_ids, route_weight, w_up, w_down):
    groups = lax.axis_size("group")
    inner_size = lax.axis_size("inner")
    count_rows = pair_rows.shape[0]
    model_width = pair_rows.shape[1]
    local_count = w_up.shape[0]
    capacity = 2 * count_rows // groups
    group_of = group_ids[:, 0]
    onehot = (group_of[:, None] == jnp.arange(groups, dtype=jnp.int32)[None, :]).astype(jnp.int32)
    rank_in = jnp.sum((jnp.cumsum(onehot, 0) - onehot) * onehot, 1)
    target = group_of * capacity + rank_in
    placing = (jnp.arange(groups * capacity, dtype=jnp.int32)[:, None] == target[None, :]).astype(
        jnp.bfloat16
    )
    outgoing = jnp.dot(placing, pair_rows, preferred_element_type=jnp.float32).astype(jnp.bfloat16)
    outgoing = outgoing.reshape(1, groups, capacity, model_width)
    tag_rows = (local_ids[:, 0] + 1).astype(jnp.bfloat16)
    tags = jnp.dot(placing, tag_rows, preferred_element_type=jnp.float32).astype(jnp.bfloat16)
    tags = tags.reshape(1, groups, capacity)
    arrived, arrived_tags = (
        lax.all_to_all(outgoing, "group", split_axis=1, concat_axis=1, tiled=True),
        lax.all_to_all(tags, "group", split_axis=1, concat_axis=1, tiled=True),
    )
    gathered, gathered_tags = (
        lax.all_gather(arrived, "inner", axis=0, tiled=True),
        lax.all_gather(arrived_tags, "inner", axis=0, tiled=True),
    )
    slots = gathered.reshape(inner_size * groups * capacity, model_width)
    slot_tags = gathered_tags.reshape(inner_size * groups * capacity).astype(jnp.float32)
    expert_index = jnp.arange(local_count, dtype=jnp.float32) + 1.0
    own_rows = groups * capacity
    selector = (slot_tags[:, None] == expert_index[None, :]).astype(jnp.float32)
    up_val = jnp.einsum("rd,edf->ref", slots, w_up, preferred_element_type=jnp.float32)
    hidden = (jax.nn.silu(up_val) * selector[:, :, None]).astype(jnp.bfloat16)
    every_term = jnp.einsum("ref,efd->rd", hidden, w_down, preferred_element_type=jnp.float32)
    totals = lax.psum(every_term.astype(jnp.bfloat16), "inner").astype(jnp.float32)
    summed = lax.dynamic_slice_in_dim(totals, lax.axis_index("inner") * own_rows, own_rows, 0)
    send_back = summed.astype(jnp.bfloat16).reshape(groups, capacity, model_width)
    returned = lax.all_to_all(send_back, "group", split_axis=0, concat_axis=0, tiled=True)
    combined = jnp.dot(
        placing.T,
        returned.reshape(groups * capacity, model_width),
        preferred_element_type=jnp.float32,
    )
    return (combined * route_weight[:, None]).astype(jnp.bfloat16)


def solution(mesh):
    placed = (
        P(("group", "inner"), None),
        P(("group", "inner"), None),
        P(("group", "inner"), None),
        P(("group", "inner")),
        P("group", None, "inner"),
        P("group", "inner", None),
    )
    return jax.shard_map(
        body, mesh=mesh, in_specs=placed, out_specs=P(("group", "inner"), None), check_vma=False
    )
```

profile of v0, /device:TPU:1, one launch (start us, length us, event | category | flops | bytes accessed | tf_op | source)
XLA Modules:
  0.0 338.9 jit_solution(1572055282033931939)
XLA Ops:
  6.5 0.0 copy-start
  6.5 0.0 all-gather.2.cloned.1.call-start
  6.5 0.9 fusion.5
  7.5 0.8 select_reduce_fusion
  8.3 0.7 multiply_add_fusion
  9.0 1.0 convolution_convert_fusion
  10.0 0.1 reshape.67
  10.1 18.5 %all_to_all.15 = bf16[1,16,2,2048]{3,2,0,1:T(2,128)(2,1)S(1)} all-to-all(bf16[1,16,2,2048]{3,2,0,1:T(2,128)(2,1)S(1)} %bitcast.15), channel_id=1, replica_groups=mesh['group'=16,'inner'=32] {'group'}, dimensions={1} | all-to-all | bytes 262144 | tf_op jit(solution)/shard_map/all_to_all | solution.py:27
  28.6 0.7 copy.14
  29.2 0.0 all-gather.2.cloned.1.call-update
  29.3 0.8 fusion.1
  30.1 0.7 reshape.78
  30.8 3.4 all-to-all-start.1
  34.1 0.0 all-reduce.2.cloned.1.call-start
  34.2 6.5 %all-to-all-done.1 = bf16[1,16,2]{2,0,1:T(2,128)(2,1)S(1)} async-done(((bf16[1,16,2]{2,0,1:T(2,128)(2,1)}), bf16[1,16,2]{2,0,1:T(2,128)(2,1)S(1)}, u32[]{:S(2)}, u32[]{:S(2)}) %all-to-all-start.1) | async-done | bytes 96 | tf_op jit(solution)/shard_map/all_to_all | solution.py:28
  40.7 0.1 copy.17
  40.8 37.2 %all_gather.7 = bf16[32,16,2]{1,2,0:T(2,128)(2,1)S(1)} all-gather(bf16[1,16,2]{1,2,0:T(2,128)(2,1)S(1)} %copy.17), channel_id=1, replica_groups=mesh['group'=16,'inner'=32] {'inner'}, dimensions={0}, use_global_device_ids=true | all-gather | bytes 2112 | tf_op jit(solution)/shard_map/all_gather | solution.py:32
  78.0 0.1 copy.18
  78.1 0.2 copy.19
  78.3 0.2 reshape.72
  78.5 0.1 compare_convert_fusion
  78.5 34.5 %all-gather.2.cloned.1.call-done = bf16[32,16,2,2048]{3,1,2,0:T(8,128)(2,1)} async-done(((bf16[1,16,2,2048]{3,1,2,0:T(8,128)(2,1)}), bf16[32,16,2,2048]{3,1,2,0:T(8,128)(2,1)}) %all-gather.2.cloned.1.call-update) | async-done | bytes 4194320 | tf_op jit(solution)/shard_map/all_gather | solution.py:31
  113.1 8.5 %copy.15 = bf16[32,16,2,2048]{3,2,1,0:T(2,128)(2,1)} copy(bf16[32,16,2,2048]{3,1,2,0:T(8,128)(2,1)} %all-gather.2.cloned.1.call-done) | data formatting | bytes 8388608 | tf_op jit(solution)/shard_map/all_gather | solution.py:31
  121.6 7.2 %reshape.73 = bf16[1024,2048,1]{1,0,2:T(8,128)(2,1)} reshape(bf16[32,16,2,2048]{3,2,1,0:T(2,128)(2,1)} %copy.15) | data formatting | bytes 8388608 | tf_op jit(solution)/shard_map/reshape | solution.py:34
  128.8 0.0 copy-done
  128.8 9.5 %bitcast_convert_fusion = bf16[1024,2048]{1,0:T(8,128)(2,1)} fusion(bf16[2,256,2048]{2,1,0:T(8,128)(2,1)S(1)} %copy-done, bf16[1024,2048,1]{1,0,2:T(8,128)(2,1)} %reshape.73, bf16[2,2048,256]{2,1,0:T(8,128)(2,1)} %param.10, f32[1024,2]{0,1:T(2,128)S(1)} %compare_convert_fusion), kind=kOutput, calls=%fused_computation | convolution fusion | flops 4300210176 | bytes 12591104 | tf_op jit(solution)/shard_map/ref,efd->rd/dot_general | solution.py:41
  138.3 0.0 copy-start.1
  138.3 0.0 all-reduce.2.cloned.1.call-update
  138.4 172.9 %all-reduce.2.cloned.1.call-done = bf16[1024,2048]{1,0:T(8,128)(2,1)} async-done(((bf16[1024,2048]{1,0:T(8,128)(2,1)}), bf16[1024,2048]{1,0:T(8,128)(2,1)}) %all-reduce.2.cloned.1.call-update) | async-done | bytes 4194320 | tf_op jit(solution)/shard_map/psum | solution.py:42
  311.2 0.9 convert_convert_fusion
  312.1 0.1 reshape.70
  312.2 19.0 %all_to_all.16 = bf16[16,2,2048]{2,1,0:T(2,128)(2,1)S(1)} all-to-all(bf16[16,2,2048]{2,1,0:T(2,128)(2,1)S(1)} %reshape.70), channel_id=1, replica_groups=mesh['group'=16,'inner'=32] {'group'}, dimensions={0} | all-to-all | bytes 262144 | tf_op jit(solution)/shard_map/all_to_all | solution.py:45
  331.2 0.1 reshape.71
  331.2 0.0 copy-done.1
  331.3 0.8 fusion
  (2 shorter events, 0.0 us)
Async XLA Ops:
  6.5 122.3 %copy-start = (bf16[2,256,2048]{2,1,0:T(8,128)(2,1)S(1)}, bf16[2,256,2048]{2,1,0:T(8,128)(2,1)}, u32[]{:S(2)}) copy-start(bf16[2,256,2048]{2,1,0:T(8,128)(2,1)} %param.11) | copy-start | bytes 6291460
  6.5 106.6 %all-gather.2.cloned.1.call-start = ((), (), s32[]{:S(2)}) async-start(), calls=%async_computation.3 | async-start | bytes 4325376 | tf_op jit(solution)/shard_map/all_gather | solution.py:31
  30.8 9.9 %all-to-all-start.1 = ((bf16[1,16,2]{2,0,1:T(2,128)(2,1)}), bf16[1,16,2]{2,0,1:T(2,128)(2,1)S(1)}, u32[]{:S(2)}, u32[]{:S(2)}) async-start(bf16[1,16,2]{2,0,1:T(2,128)(2,1)} %reshape.78), calls=%async_computation.1 | async-start | bytes 16384 | tf_op jit(solution)/shard_map/all_to_all | solution.py:28
  34.1 277.1 %all-reduce.2.cloned.1.call-start = ((), (), s32[]{:S(2)}) async-start(), calls=%async_computation.4 | async-start | bytes 8388608 | tf_op jit(solution)/shard_map/psum | solution.py:42
  138.3 192.9 %copy-start.1 = (f32[16]{0:T(128)S(1)}, f32[16]{0:T(128)}, u32[]{:S(2)}) copy-start(f32[16]{0:T(128)} %param.9) | copy-start | bytes 196
Sparse Core Ops, SparseCore 0:
  29.4 83.6 all-gather.1
  138.5 172.6 all-reduce.1
where the time goes:
time: 339 us
  waiting for transfers between devices  214 us (63%)
  blocking collectives  74.7 us (22%)
  local copies, waits for them, and re-layouts  17.9 us (5%)
  between operations  13.5 us (4%)
  matrix products  12.1 us (4%)
  starting transfers between devices  3.41 us (1%)
  other arithmetic  3.41 us (1%)
    psum x1, waiting for transfers between devices, body(): lax.psum(every_term.astype(jnp.bfloat16), 'inner').astype(jnp.float32)  173 us
    all_gather x1, blocking collectives, body(): lax.all_gather(arrived_tags, 'inner', axis=0, tiled=True)  37.2 us
    all_gather x1, waiting for transfers between devices, body(): lax.all_gather(arrived, 'inner', axis=0, tiled=True)  34.5 us
    all_to_all x1, blocking collectives, body(): lax.all_to_all(send_back, 'group', split_axis=0, concat_axis=0, tiled=True)  19 us
    all_to_all x1, blocking collectives, body(): lax.all_to_all(outgoing, 'group', split_axis=1, concat_axis=1, tiled=True)  18.5 us
    dot_general x1, matrix products, body(): jnp.einsum('ref,efd->rd', hidden, w_down, preferred_element_type=jnp.floa...  9.51 us
    all_gather x1, local copies, waits for them, and re-layouts, body(): lax.all_gather(arrived, 'inner', axis=0, tiled=True)  8.52 us
    reshape x1, local copies, waits for them, and re-layouts, body(): slots = gathered.reshape(inner_size * groups * capacity, model_width)  7.19 us
  transfers between devices with their start and end apart: 3, of which 3 were waited for; matrix products, arithmetic and copies ran while one was open for 1% of the time, Pallas kernels for 0%

commit v1 on v0

--- a/solution.py
+++ b/solution.py
@@ -28,7 +28,9 @@
         lax.all_to_all(tags, "group", split_axis=1, concat_axis=1, tiled=True),
     )
     gathered, gathered_tags = (
-        lax.all_gather(arrived, "inner", axis=0, tiled=True),
+        jnp.concatenate(
+            lax.all_to_all(jnp.stack([arrived] * lax.axis_size("inner")), "inner", 0, 0), axis=0
+        ),
         lax.all_gather(arrived_tags, "inner", axis=0, tiled=True),
     )
     slots = gathered.reshape(inner_size * groups * capacity, model_width)

time: 339 us -> 394 us (1.16)
  blocking collectives: 74.7 us -> 149 us
  waiting for transfers between devices: 214 us -> 178 us
  starting transfers between devices: 3.41 us -> 21.6 us
    all_gather x1, blocking collectives: 37.2 us -> 118 us  [body(): lax.all_gather(arrived_tags, 'inner', axis=0, tiled=True)]
    all_gather x1 -> x0, waiting for transfers between devices: 34.5 us -> none  [body(): lax.all_gather(arrived, 'inner', axis=0, tiled=True)]
    another operation x0 -> x2, local copies, waits for them, and re-layouts: none -> 13.1 us  [the longest x1 7.21 us: body(): slots = gathered.reshape(inner_size * groups * capacity, model_width)]
    all_to_all x0 -> x1, starting transfers between devices: none -> 11.4 us  [body(): lax.all_to_all(jnp.stack([arrived] * lax.axis_size('inner')), 'inner', 0, 0)]
    all_gather x1 -> x0, local copies, waits for them, and re-layouts: 8.52 us -> none  [body(): lax.all_gather(arrived, 'inner', axis=0, tiled=True)]
    reshape x1 -> x0, local copies, waits for them, and re-layouts: 7.19 us -> none  [body(): slots = gathered.reshape(inner_size * groups * capacity, model_width)]
    all_to_all x1, starting transfers between devices: 3.37 us -> 10.1 us  [body(): lax.all_to_all(tags, 'group', split_axis=1, concat_axis=1, tiled=True)]
    all_to_all x1, blocking collectives: 18.5 us -> 12.3 us  [body(): lax.all_to_all(outgoing, 'group', split_axis=1, concat_axis=1, tiled=True)]
  transfers between devices with their start and end apart: 3 -> 3, of which waited for: 3 -> 2; matrix products, arithmetic and copies ran while one was open for 1% -> 0% of each run, Pallas kernels for 0% -> 0%
where the time goes in v1:
time: 394 us; the launch traced here: 393 us
  waiting for transfers between devices  178 us (45%)
  blocking collectives  149 us (38%)
  starting transfers between devices  21.6 us (5%)
  local copies, waits for them, and re-layouts  14.6 us (4%)
  between operations  13.5 us (3%)
  matrix products  12.1 us (3%)
    psum x1, waiting for transfers between devices, body(): lax.psum(every_term.astype(jnp.bfloat16), 'inner').astype(jnp.float32)  173 us
    all_gather x1, blocking collectives, body(): lax.all_gather(arrived_tags, 'inner', axis=0, tiled=True)  118 us
    all_to_all x1, blocking collectives, body(): lax.all_to_all(send_back, 'group', split_axis=0, concat_axis=0, tiled=True)  19 us
    all_to_all x1, blocking collectives, body(): lax.all_to_all(outgoing, 'group', split_axis=1, concat_axis=1, tiled=True)  12.3 us
    all_to_all x1, starting transfers between devices, body(): lax.all_to_all(jnp.stack([arrived] * lax.axis_size('inner')), 'inner', 0, 0)  11.4 us
    all_to_all x1, starting transfers between devices, body(): lax.all_to_all(tags, 'group', split_axis=1, concat_axis=1, tiled=True)  10.1 us
    dot_general x1, matrix products, body(): jnp.einsum('ref,efd->rd', hidden, w_down, preferred_element_type=jnp.floa...  9.5 us
  transfers between devices with their start and end apart: 3, of which 2 were waited for; matrix products, arithmetic and copies ran while one was open for 0% of the time, Pallas kernels for 0%

profile of v1, /device:TPU:1, one launch (start us, length us, event | category | flops | bytes accessed | tf_op | source)
XLA Modules:
  0.0 393.1 jit_solution(7480798774100154387)
XLA Ops:
  6.5 0.0 copy-start
  6.5 0.9 fusion.5
  7.4 0.8 select_reduce_fusion
  8.3 0.7 multiply_add_fusion
  8.9 0.8 fusion.1
  9.7 0.7 reshape.77
  10.4 10.1 %all-to-all-start.2 = ((bf16[1,16,2]{2,0,1:T(2,128)(2,1)}), bf16[1,16,2]{2,0,1:T(2,128)(2,1)S(1)}, u32[]{:S(2)}, u32[]{:S(2)}) async-start(bf16[1,16,2]{2,0,1:T(2,128)(2,1)} %reshape.77), calls=%async_computation.2 | async-start | bytes 16384 | tf_op jit(solution)/shard_map/all_to_all | solution.py:28
  20.6 1.0 convolution_convert_fusion
  21.6 0.1 reshape.67
  21.7 5.9 %all-to-all-done.2 = bf16[1,16,2]{2,0,1:T(2,128)(2,1)S(1)} async-done(((bf16[1,16,2]{2,0,1:T(2,128)(2,1)}), bf16[1,16,2]{2,0,1:T(2,128)(2,1)S(1)}, u32[]{:S(2)}, u32[]{:S(2)}) %all-to-all-start.2) | async-done | bytes 96 | tf_op jit(solution)/shard_map/all_to_all | solution.py:28
  27.6 12.3 %all_to_all.23 = bf16[1,16,2,2048]{3,2,0,1:T(2,128)(2,1)S(1)} all-to-all(bf16[1,16,2,2048]{3,2,0,1:T(2,128)(2,1)S(1)} %bitcast.17), channel_id=1, replica_groups=mesh['group'=16,'inner'=32] {'group'}, dimensions={1} | all-to-all | bytes 262144 | tf_op jit(solution)/shard_map/all_to_all | solution.py:27
  39.8 5.9 %stack.2 = bf16[32,1,16,2,2048]{4,3,2,1,0:T(2,128)(2,1)} broadcast(bf16[16,2,2048]{2,1,0:T(2,128)(2,1)S(1)} %bitcast.16), dimensions={2,3,4} | broadcast | bytes 4325376 | tf_op jit(solution)/shard_map/stack | solution.py:32
  45.7 11.4 %all-to-all-start.1 = ((bf16[32,1,16,2,2048]{4,3,2,1,0:T(2,128)(2,1)}), bf16[32,1,16,2,2048]{4,3,2,1,0:T(2,128)(2,1)}, u32[]{:S(2)}, u32[]{:S(2)}) async-start(bf16[32,1,16,2,2048]{4,3,2,1,0:T(2,128)(2,1)} %stack.2), calls=%async_computation.1 | async-start | bytes 8388608 | tf_op jit(solution)/shard_map/all_to_all | solution.py:32
  57.2 0.0 all-reduce.2.cloned.1.call-start
  57.2 0.1 copy.13
  57.3 118.1 %all_gather.3 = bf16[32,16,2]{1,2,0:T(2,128)(2,1)S(1)} all-gather(bf16[1,16,2]{1,2,0:T(2,128)(2,1)S(1)} %copy.13), channel_id=1, replica_groups=mesh['group'=16,'inner'=32] {'inner'}, dimensions={0}, use_global_device_ids=true | all-gather | bytes 2112 | tf_op jit(solution)/shard_map/all_gather | solution.py:34
  175.5 0.1 copy.14
  175.5 0.2 copy.15
  175.8 0.2 reshape.71
  175.9 0.1 compare_convert_fusion
  176.0 0.0 all-to-all-done.1
  176.0 7.2 %reshape.72 = bf16[1024,2048,1]{1,0,2:T(8,128)(2,1)} reshape(bf16[32,1,16,2,2048]{4,3,2,1,0:T(2,128)(2,1)} %all-to-all-done.1) | data formatting | bytes 8388608 | tf_op jit(solution)/shard_map/reshape;reshape | solution.py:36
  183.2 0.0 copy-done
  183.2 9.5 %bitcast_convert_fusion = bf16[1024,2048]{1,0:T(8,128)(2,1)} fusion(bf16[2,256,2048]{2,1,0:T(8,128)(2,1)S(1)} %copy-done, bf16[1024,2048,1]{1,0,2:T(8,128)(2,1)} %reshape.72, bf16[2,2048,256]{2,1,0:T(8,128)(2,1)} %param.10, f32[1024,2]{0,1:T(2,128)S(1)} %compare_convert_fusion), kind=kOutput, calls=%fused_computation | convolution fusion | flops 4300210176 | bytes 12591104 | tf_op jit(solution)/shard_map/ref,efd->rd/dot_general | solution.py:43
  192.7 0.0 copy-start.1
  192.7 0.0 all-reduce.2.cloned.1.call-update
  192.7 172.6 %all-reduce.2.cloned.1.call-done = bf16[1024,2048]{1,0:T(8,128)(2,1)} async-done(((bf16[1024,2048]{1,0:T(8,128)(2,1)}), bf16[1024,2048]{1,0:T(8,128)(2,1)}) %all-reduce.2.cloned.1.call-update) | async-done | bytes 4194320 | tf_op jit(solution)/shard_map/psum | solution.py:44
  365.3 0.9 convert_convert_fusion
  366.2 0.1 reshape.69
  366.4 19.0 %all_to_all.24 = bf16[16,2,2048]{2,1,0:T(2,128)(2,1)S(1)} all-to-all(bf16[16,2,2048]{2,1,0:T(2,128)(2,1)S(1)} %reshape.69), channel_id=1, replica_groups=mesh['group'=16,'inner'=32] {'group'}, dimensions={0} | all-to-all | bytes 262144 | tf_op jit(solution)/shard_map/all_to_all | solution.py:47
  385.3 0.1 reshape.70
  385.4 0.0 copy-done.1
  385.4 0.8 fusion
  (2 shorter events, 0.0 us)
Async XLA Ops:
  6.5 176.7 %copy-start = (bf16[2,256,2048]{2,1,0:T(8,128)(2,1)S(1)}, bf16[2,256,2048]{2,1,0:T(8,128)(2,1)}, u32[]{:S(2)}) copy-start(bf16[2,256,2048]{2,1,0:T(8,128)(2,1)} %param.11) | copy-start | bytes 6291460
  10.4 17.1 %all-to-all-start.2 = ((bf16[1,16,2]{2,0,1:T(2,128)(2,1)}), bf16[1,16,2]{2,0,1:T(2,128)(2,1)S(1)}, u32[]{:S(2)}, u32[]{:S(2)}) async-start(bf16[1,16,2]{2,0,1:T(2,128)(2,1)} %reshape.77), calls=%async_computation.2 | async-start | bytes 16384 | tf_op jit(solution)/shard_map/all_to_all | solution.py:28
  45.7 130.3 %all-to-all-start.1 = ((bf16[32,1,16,2,2048]{4,3,2,1,0:T(2,128)(2,1)}), bf16[32,1,16,2,2048]{4,3,2,1,0:T(2,128)(2,1)}, u32[]{:S(2)}, u32[]{:S(2)}) async-start(bf16[32,1,16,2,2048]{4,3,2,1,0:T(2,128)(2,1)} %stack.2), calls=%async_computation.1 | async-start | bytes 8388608 | tf_op jit(solution)/shard_map/all_to_all | solution.py:32
  57.2 308.2 %all-reduce.2.cloned.1.call-start = ((), (), s32[]{:S(2)}) async-start(), calls=%async_computation.4 | async-start | bytes 8388608 | tf_op jit(solution)/shard_map/psum | solution.py:44
  192.7 192.7 %copy-start.1 = (f32[16]{0:T(128)S(1)}, f32[16]{0:T(128)}, u32[]{:S(2)}) copy-start(f32[16]{0:T(128)} %param.9) | copy-start | bytes 196
Sparse Core Ops, SparseCore 0:
  192.9 172.4 all-reduce.1
